TPU v7x, 1024 devices: a whole 4x8x16 slice. The times are simulated.
1024 devices in a mesh: gx: 8 (over z_lo), gy: 16 (over y, core), gz: 8 (over x, z_hi).
Axes of the slice: x: 4, y: 8, z: 16 (z_hi: 2, z_lo: 8; z = z_hi * 8 + z_lo), core: 2. Of those that a mesh axis runs over, the one named last changes fastest.
Arguments:
- states: bfloat16 [192, 983040], P(None, ('gx', 'gy', 'gz')), may hold values from -16 to 16
- cell_matrices: bfloat16 [2048, 512, 512], P(('gx', 'gy', 'gz')), as said below
- connectivity: int32 [2048, 512], P(('gx', 'gy', 'gz')), may hold values from 0 to 959, as said below
- side_nodes: int32 [4, 122880], P(None, ('gx', 'gy', 'gz')), may hold values from 0 to 959, as said below
- top_nodes: int32 [2, 65536], P(None, ('gx', 'gy', 'gz')), may hold values from 0 to 959, as said below
- pot_index: int32 [983040], P(('gx', 'gy', 'gz')), may hold values from 0 to 63
- pot_table: float32 [64], replicated, may hold values from -1 to 1
Outputs:
- rotated: bfloat16 [192, 983040], P(None, ('gx', 'gy', 'gz'))
Inputs may be any that keep to these rules, and one draw needn't show every extreme that they name: `connectivity`: slot numbers within one block; the nodes of one element take distinct slots. `side_nodes`: slot numbers within one block. `top_nodes`: slot numbers within one block. `cell_matrices`: each element's matrix is symmetric.
All inputs are finite; a program needn't handle non-finite values.
Results may differ from a plain program's by a relative error of at most 0.0067.
Values sent between devices are 32-bit elements; how exact they have to be, the bound alone decides.
A program may use at most 32 MiB of HBM per device.

v0:
```python
import jax
import jax.numpy as jnp
from jax import lax
from jax.sharding import PartitionSpec as P


def with_halo(array, sides, width):
    for axis, dim in sides:
        size, length = (lax.axis_size(axis), array.shape[dim])
        up = [(i, (i + 1) % size) for i in range(size - 1)]
        down = [(j, i) for i, j in up]
        last = lax.slice_in_dim(array, length - width, length, axis=dim)
        first = lax.slice_in_dim(array, 0, width, axis=dim)
        before = lax.ppermute(last, axis, up)
        after = lax.ppermute(first, axis, down)
        array = jnp.concatenate([before, array, after], axis=dim)
    return array


def in_blocks(array, dim, size):
    before, after = (array.shape[:dim], array.shape[dim + 1 :])
    return jnp.moveaxis(array.reshape(*before, size, -1, *after), dim, 0)


def sum_at_owner(array, axis, dim):
    pieces = in_blocks(array, dim, lax.axis_size(axis))
    arrived = lax.all_to_all(pieces, axis, split_axis=0, concat_axis=0, tiled=True)
    return arrived.sum(axis=0)


def from_everyone(array, axis):
    size = lax.axis_size(axis)
    return lax.all_to_all(
        jnp.broadcast_to(array[None], (size, *array.shape)), axis, 0, 0, tiled=True
    )


def over_copies(array, axis):
    everything = from_everyone(array, axis)
    return jnp.sum(everything, axis=0)


def in_order(pieces, dim):
    pieces = jnp.moveaxis(pieces, 0, dim)
    shape = pieces.shape
    return pieces.reshape(*shape[:dim], shape[dim] * shape[dim + 1], *shape[dim + 2 :])


def gathered_copies(array, axis, dim):
    pieces = from_everyone(array, axis)
    return in_order(pieces, dim)


def on_device(states, cell_matrices, connectivity, side_nodes, top_nodes, pot_index, pot_table):
    width = states.shape[0]
    slots = states.shape[1]
    cells = cell_matrices.shape[0]
    corner = cell_matrices.shape[1]
    flat_conn = connectivity.reshape(-1)
    levels = lax.broadcasted_iota(jnp.int32, (pot_table.shape[0], slots), 0)
    potential = jnp.sum(jnp.where(levels == pot_index[None, :], pot_table[:, None], 0.0), axis=0)
    face_lists = (
        (side_nodes[0], side_nodes[1]),
        (side_nodes[2], side_nodes[3]),
        (top_nodes[0], top_nodes[1]),
    )
    face_slots = jnp.concatenate(
        [
            face_lists[0][0],
            face_lists[1][0],
            face_lists[2][0],
            face_lists[0][1],
            face_lists[1][1],
            face_lists[2][1],
        ]
    )

    def cell_sum(field):
        rounded = field.astype(jnp.bfloat16)
        cols = jnp.take(rounded, flat_conn, axis=1).reshape(width, cells, corner)
        prod = jnp.einsum("cij,scj->sci", cell_matrices, cols, preferred_element_type=jnp.float32)
        zeros = jnp.zeros((width, slots), jnp.float32)
        return zeros.at[:, flat_conn].add(prod.reshape(width, cells * corner))

    def pair(values, direction):
        low_list, up_list = face_lists[direction]
        return jnp.stack([values[:, low_list], values[:, up_list]])

    def apply(field):
        cellsum = cell_sum(field)
        got_first = with_halo(pair(cellsum, 0), (("gx", 0),), 1)
        got_second = with_halo(pair(cellsum, 1), (("gy", 0),), 1)
        got_third = with_halo(pair(cellsum, 2), (("gz", 0),), 1)
        received = jnp.concatenate(
            [got_first[0], got_second[0], got_third[0], got_first[3], got_second[3], got_third[3]],
            axis=1,
        )
        total = cellsum.at[:, face_slots].add(received)
        return total + potential[None, :] * field

    start = states.astype(jnp.float32)
    first = (apply(start) - 0.5 * start) / 3.0
    filtered = (2.0 * (apply(first) - 0.5 * first) / 3.0 - start).astype(jnp.bfloat16)
    partial_gram = jnp.dot(filtered, filtered.T, preferred_element_type=jnp.float32)
    rows_part = sum_at_owner(partial_gram, "gy", 0)
    rows_part = over_copies(rows_part, ("gx", "gz"))
    correlation = gathered_copies(rows_part, "gy", 0)
    total_slots = slots * lax.axis_size("gx") * lax.axis_size("gy") * lax.axis_size("gz")
    correlation = correlation / total_slots
    lower = jnp.linalg.cholesky(correlation)
    inverse = jax.scipy.linalg.solve_triangular(
        lower, jnp.eye(width, dtype=jnp.float32), lower=True
    )
    inverse = inverse.astype(jnp.bfloat16)
    return jnp.dot(inverse, filtered, preferred_element_type=jnp.float32).astype(jnp.bfloat16)


def solution(mesh):
    in_specs = (
        P(None, ("gx", "gy", "gz")),
        P(("gx", "gy", "gz"), None, None),
        P(("gx", "gy", "gz"), None),
        P(None, ("gx", "gy", "gz")),
        P(None, ("gx", "gy", "gz")),
        P(("gx", "gy", "gz")),
        P(),
    )
    out_specs = P(None, ("gx", "gy", "gz"))
    return jax.shard_map(
        on_device, mesh=mesh, in_specs=in_specs, out_specs=out_specs, check_vma=False
    )
```

profile of v0, /device:TPU:1, one launch (start us, length us, event | category | flops | bytes accessed | tf_op | source)
XLA Modules:
  0.0 307.6 jit_solution(5606838356653681706)
XLA Ops:
  2.0 3.9 %gather_fusion.12 = bf16[1024,192]{1,0:T(8,128)(2,1)S(1)} fusion(bf16[192,960]{0,1:T(8,128)(2,1)S(1)} %copy.43, s32[1024]{0:T(1024)S(1)} %fusion.22), kind=kCustom, calls=%fused_computation.clone | custom fusion | bytes 790528 | tf_op jit(solution)/shard_map/jit(_take)/gather | solution.py:80
  8.8 6.8 %scatter_custom_fusion = f32[192,960]{0,1:T(8,128)S(1)} fusion(s32[1024]{0:T(1024)S(1)} %bitcast.177, f32[1024,192]{1,0:T(8,128)} %copy.46, f32[]{:T(128)} %constant.111.clone.1), kind=kCustom, calls=%fused_computation.40 | custom fusion | flops 196608 | bytes 737792 | tf_op jit(solution)/shard_map/scatter-add | solution.py:83
  15.6 1.4 gather_fusion
  17.0 5.4 %collective-permute-start = (f32[1,192,120]{1,2,0:T(8,128)}, f32[1,192,120]{1,2,0:T(8,128)}, u32[]{:S(2)}, u32[]{:S(2)}) collective-permute-start(f32[1,192,120]{1,2,0:T(8,128)} %bitcast.13), channel_id=1, source_target_pairs={{0,128},{128,256},{256,384},{384,512},{512,640},{640,768},{768,896... | collective-permute-start | bytes 276488 | tf_op jit(solution)/shard_map/ppermute | solution.py:14
  23.8 4.2 %collective-permute-start.1 = (f32[1,192,120]{1,2,0:T(8,128)}, f32[1,192,120]{1,2,0:T(8,128)}, u32[]{:S(2)}, u32[]{:S(2)}) collective-permute-start(f32[1,192,120]{1,2,0:T(8,128)} %bitcast.17), channel_id=1, source_target_pairs={{0,8},{8,16},{16,24},{24,32},{32,40},{40,48},{48,56},{56,64},{64,7... | collective-permute-start | bytes 276488 | tf_op jit(solution)/shard_map/ppermute | solution.py:14
  29.3 18.8 %collective-permute-start.2 = (f32[1,192,64]{1,2,0:T(8,128)}, f32[1,192,64]{1,2,0:T(8,128)}, u32[]{:S(2)}, u32[]{:S(2)}) collective-permute-start(f32[1,192,64]{1,2,0:T(8,128)} %bitcast.21), channel_id=1, source_target_pairs={{0,1},{1,2},{2,3},{3,4},{4,5},{5,6},{6,7},{8,9},{9,10},{10,11},{11... | collective-permute-start | bytes 147464 | tf_op jit(solution)/shard_map/ppermute | solution.py:14
  48.1 1.4 gather_fusion.3
  50.8 1.4 gather_fusion.4
  52.1 2.0 collective-permute-start.4
  64.3 8.3 %collective-permute-done.5 = f32[1,192,64]{1,2,0:T(8,128)S(1)} collective-permute-done((f32[1,192,64]{1,2,0:T(8,128)}, f32[1,192,64]{1,2,0:T(8,128)S(1)}, u32[]{:S(2)}, u32[]{:S(2)}) %collective-permute-start.5) | collective-permute-done | bytes 49184 | tf_op jit(solution)/shard_map/ppermute | solution.py:15
  72.6 6.5 %scatter_custom_fusion.1 = f32[192,960]{0,1:T(8,128)S(1)} fusion(f32[192,960]{0,1:T(8,128)S(1)} %fusion, s32[608]{0:T(1024)S(1)} %fusion.23, f32[192,608]{0,1:T(8,128)S(1)} %bitcast_dynamic-update-slice_fusion.10), kind=kCustom, calls=%fused_computation.34 | custom fusion | flops 116736 | bytes 1359872 | tf_op jit(solution)/shard_map/scatter-add | solution.py:98
  79.2 4.9 %gather_fusion.13 = bf16[1024,192]{1,0:T(8,128)(2,1)} fusion(bf16[192,960]{0,1:T(8,128)(2,1)S(1)} %multiply_convert_fusion, s32[1024]{0:T(1024)S(1)} %fusion.22), kind=kCustom, calls=%fused_computation.1.clone | custom fusion | bytes 790528 | tf_op jit(solution)/shard_map/jit(_take)/gather | solution.py:80
  87.4 6.8 %scatter_custom_fusion.2 = f32[192,960]{0,1:T(8,128)S(1)} fusion(s32[1024]{0:T(1024)S(1)} %bitcast.178, f32[1024,192]{1,0:T(8,128)} %copy.50, f32[]{:T(128)} %constant.111.clone.1), kind=kCustom, calls=%fused_computation.38 | custom fusion | flops 196608 | bytes 737792 | tf_op jit(solution)/shard_map/scatter-add | solution.py:83
  94.1 1.4 gather_fusion.6
  95.5 5.9 %collective-permute-start.6 = (f32[1,192,120]{1,2,0:T(8,128)}, f32[1,192,120]{1,2,0:T(8,128)}, u32[]{:S(2)}, u32[]{:S(2)}) collective-permute-start(f32[1,192,120]{1,2,0:T(8,128)} %bitcast.171), channel_id=1, source_target_pairs={{0,128},{128,256},{256,384},{384,512},{512,640},{640,768},{768,896... | collective-permute-start | bytes 276488 | tf_op jit(solution)/shard_map/ppermute | solution.py:14
  102.7 1.4 gather_fusion.7
  106.7 1.4 gather_fusion.10
  109.4 5.7 %collective-permute-start.7 = (f32[1,192,120]{1,2,0:T(8,128)}, f32[1,192,120]{1,2,0:T(8,128)S(1)}, u32[]{:S(2)}, u32[]{:S(2)}) collective-permute-start(f32[1,192,120]{1,2,0:T(8,128)} %bitcast.170), channel_id=1, source_target_pairs={{0,8},{8,16},{16,24},{24,32},{32,40},{40,48},{48,56},{56,64},{64,7... | collective-permute-start | bytes 276488 | tf_op jit(solution)/shard_map/ppermute | solution.py:14
  115.0 1.7 collective-permute-start.8
  118.0 1.9 collective-permute-start.10
  122.2 4.1 %collective-permute-done.9 = f32[1,192,120]{1,2,0:T(8,128)S(1)} collective-permute-done((f32[1,192,120]{1,2,0:T(8,128)}, f32[1,192,120]{1,2,0:T(8,128)S(1)}, u32[]{:S(2)}, u32[]{:S(2)}) %collective-permute-start.9) | collective-permute-done | bytes 92192 | tf_op jit(solution)/shard_map/ppermute | solution.py:15
  126.4 7.8 %collective-permute-done.11 = f32[1,192,64]{1,2,0:T(8,128)S(1)} collective-permute-done((f32[1,192,64]{1,2,0:T(8,128)}, f32[1,192,64]{1,2,0:T(8,128)S(1)}, u32[]{:S(2)}, u32[]{:S(2)}) %collective-permute-start.11) | collective-permute-done | bytes 49184 | tf_op jit(solution)/shard_map/ppermute | solution.py:15
  134.2 7.8 %scatter_custom_fusion.3 = f32[192,960]{0,1:T(8,128)} fusion(f32[192,960]{0,1:T(8,128)} %multiply_add_fusion, s32[608]{0:T(1024)S(1)} %fusion.23, f32[192,608]{0,1:T(8,128)S(1)} %bitcast_dynamic-update-slice_fusion.8), kind=kCustom, calls=%fused_computation.32 | custom fusion | flops 116736 | bytes 1359872 | tf_op jit(solution)/shard_map/scatter-add | solution.py:98
  141.9 1.5 fusion.2
  143.8 22.6 %all_to_all.15 = f32[16,12,192]{2,1,0:T(8,128)S(1)} all-to-all(f32[16,12,192]{2,1,0:T(8,128)S(1)} %reshape.495), channel_id=1, replica_groups=mesh['gx'=8,'gy'=16,'gz'=8] {'gy'}, dimensions={0} | all-to-all | bytes 294912 | tf_op jit(solution)/shard_map/all_to_all | solution.py:27
  166.5 70.9 %all_to_all.16 = f32[64,12,192]{2,1,0:T(8,128)S(1)} all-to-all(f32[64,12,192]{2,1,0:T(8,128)S(1)} %broadcast_in_dim.28), channel_id=1, replica_groups=mesh['gx'=8,'gy'=16,'gz'=8] {'gx','gz'}, dimensions={0} | all-to-all | bytes 1179648 | tf_op jit(solution)/shard_map/all_to_all | solution.py:33
  238.2 4.9 %all-to-all-start.2 = ((f32[16,12,192]{2,1,0:T(8,128)}), f32[16,12,192]{2,1,0:T(8,128)S(1)}, u32[]{:S(2)}, u32[]{:S(2)}) async-start(f32[16,12,192]{2,1,0:T(8,128)} %broadcast_in_dim.29), calls=%async_computation.2 | async-start | bytes 524288 | tf_op jit(solution)/shard_map/all_to_all | solution.py:33
  243.2 11.7 %all-to-all-done.2 = f32[16,12,192]{2,1,0:T(8,128)S(1)} async-done(((f32[16,12,192]{2,1,0:T(8,128)}), f32[16,12,192]{2,1,0:T(8,128)S(1)}, u32[]{:S(2)}, u32[]{:S(2)}) %all-to-all-start.2) | async-done | bytes 147488 | tf_op jit(solution)/shard_map/all_to_all | solution.py:33
  255.2 11.7 %cholesky.51 = f32[128,128]{1,0:T(8,128)S(1)} custom-call(f32[128,128]{1,0:T(8,128)S(1)} %cholesky.124), custom_call_target="Cholesky" | custom-call | tf_op jit(solution)/shard_map/jit(cholesky)/cholesky | solution.py:110
  266.9 9.8 %custom-call.15 = f32[1,128,128]{1,2,0:T(8,128)S(1)} custom-call(f32[1,128,128]{2,1,0:T(8,128)S(1)} %get-tuple-element.27), custom_call_target="InvertDiagBlocksLowerTriangular" | custom-call | tf_op jit(solution)/shard_map/jit(cholesky)/cholesky | solution.py:110
  277.1 5.8 %cholesky.110 = f32[64,64]{1,0:T(8,128)S(1)} custom-call(f32[64,64]{1,0:T(8,128)S(1)} %convolution_subtract_fusion.1), custom_call_target="Cholesky" | custom-call | tf_op jit(solution)/shard_map/jit(cholesky)/cholesky | solution.py:110
  285.9 19.7 %custom-call.16 = f32[2,128,128]{1,2,0:T(8,128)S(1)} custom-call(f32[2,128,128]{2,1,0:T(8,128)S(1)} %pad_maximum_fusion), custom_call_target="InvertDiagBlocksLowerTriangular" | custom-call | tf_op jit(solution)/shard_map/jit(_solve_triangular)/triangular_solve | solution.py:111
  (108 shorter events, 36.3 us)
Async XLA Ops:
  0.0 6.2 %copy-start = (bf16[2,512,512]{2,1,0:T(8,128)(2,1)S(1)}, bf16[2,512,512]{2,1,0:T(8,128)(2,1)}, u32[]{:S(2)}) copy-start(bf16[2,512,512]{2,1,0:T(8,128)(2,1)} %param.10) | copy-start | bytes 3145732
  6.8 1.3 copy-start.1
  8.1 0.7 copy-start.2
  17.0 41.4 %collective-permute-start = (f32[1,192,120]{1,2,0:T(8,128)}, f32[1,192,120]{1,2,0:T(8,128)}, u32[]{:S(2)}, u32[]{:S(2)}) collective-permute-start(f32[1,192,120]{1,2,0:T(8,128)} %bitcast.13), channel_id=1, source_target_pairs={{0,128},{128,256},{256,384},{384,512},{512,640},{640,768},{768,896... | collective-permute-start | bytes 276488 | tf_op jit(solution)/shard_map/ppermute | solution.py:14
  23.8 4.2 %copy-start.4 = (s32[2,64]{1,0:T(2,128)S(1)}, s32[2,64]{1,0:T(2,128)}, u32[]{:S(2)}) copy-start(s32[2,64]{1,0:T(2,128)} %param.13) | copy-start | bytes 1540
  23.8 36.9 %collective-permute-start.1 = (f32[1,192,120]{1,2,0:T(8,128)}, f32[1,192,120]{1,2,0:T(8,128)}, u32[]{:S(2)}, u32[]{:S(2)}) collective-permute-start(f32[1,192,120]{1,2,0:T(8,128)} %bitcast.17), channel_id=1, source_target_pairs={{0,8},{8,16},{16,24},{24,32},{32,40},{40,48},{48,56},{56,64},{64,7... | collective-permute-start | bytes 276488 | tf_op jit(solution)/shard_map/ppermute | solution.py:14
  29.3 32.3 %collective-permute-start.2 = (f32[1,192,64]{1,2,0:T(8,128)}, f32[1,192,64]{1,2,0:T(8,128)}, u32[]{:S(2)}, u32[]{:S(2)}) collective-permute-start(f32[1,192,64]{1,2,0:T(8,128)} %bitcast.21), channel_id=1, source_target_pairs={{0,1},{1,2},{2,3},{3,4},{4,5},{5,6},{6,7},{8,9},{9,10},{10,11},{11... | collective-permute-start | bytes 147464 | tf_op jit(solution)/shard_map/ppermute | solution.py:14
  49.5 13.0 %collective-permute-start.3 = (f32[1,192,120]{1,2,0:T(8,128)}, f32[1,192,120]{1,2,0:T(8,128)}, u32[]{:S(2)}, u32[]{:S(2)}) collective-permute-start(f32[1,192,120]{1,2,0:T(8,128)} %bitcast.25), channel_id=1, source_target_pairs={{128,0},{256,128},{384,256},{512,384},{640,512},{768,640},{896,768... | collective-permute-start | bytes 276488 | tf_op jit(solution)/shard_map/ppermute | solution.py:15
  52.1 2.6 copy-start.3
  52.1 11.2 %collective-permute-start.4 = (f32[1,192,120]{1,2,0:T(8,128)}, f32[1,192,120]{1,2,0:T(8,128)}, u32[]{:S(2)}, u32[]{:S(2)}) collective-permute-start(f32[1,192,120]{1,2,0:T(8,128)} %bitcast.29), channel_id=1, source_target_pairs={{8,0},{16,8},{24,16},{32,24},{40,32},{48,40},{56,48},{64,56},{72,6... | collective-permute-start | bytes 276488 | tf_op jit(solution)/shard_map/ppermute | solution.py:15
  54.8 0.7 copy-start.8
  57.0 0.6 copy-start.5
  57.0 0.7 copy-start.6
  57.0 0.7 copy-start.7
  58.4 14.1 %collective-permute-start.5 = (f32[1,192,64]{1,2,0:T(8,128)}, f32[1,192,64]{1,2,0:T(8,128)S(1)}, u32[]{:S(2)}, u32[]{:S(2)}) collective-permute-start(f32[1,192,64]{1,2,0:T(8,128)} %bitcast.166), channel_id=1, source_target_pairs={{1,0},{2,1},{3,2},{4,3},{5,4},{6,5},{7,6},{9,8},{10,9},{11,10},{12... | collective-permute-start | bytes 147464 | tf_op jit(solution)/shard_map/ppermute | solution.py:15
  95.5 24.4 %collective-permute-start.6 = (f32[1,192,120]{1,2,0:T(8,128)}, f32[1,192,120]{1,2,0:T(8,128)}, u32[]{:S(2)}, u32[]{:S(2)}) collective-permute-start(f32[1,192,120]{1,2,0:T(8,128)} %bitcast.171), channel_id=1, source_target_pairs={{0,128},{128,256},{256,384},{384,512},{512,640},{640,768},{768,896... | collective-permute-start | bytes 276488 | tf_op jit(solution)/shard_map/ppermute | solution.py:14
  109.4 12.8 %collective-permute-start.7 = (f32[1,192,120]{1,2,0:T(8,128)}, f32[1,192,120]{1,2,0:T(8,128)S(1)}, u32[]{:S(2)}, u32[]{:S(2)}) collective-permute-start(f32[1,192,120]{1,2,0:T(8,128)} %bitcast.170), channel_id=1, source_target_pairs={{0,8},{8,16},{16,24},{24,32},{32,40},{40,48},{48,56},{56,64},{64,7... | collective-permute-start | bytes 276488 | tf_op jit(solution)/shard_map/ppermute | solution.py:14
  115.0 7.1 %collective-permute-start.8 = (f32[1,192,64]{1,2,0:T(8,128)}, f32[1,192,64]{1,2,0:T(8,128)S(1)}, u32[]{:S(2)}, u32[]{:S(2)}) collective-permute-start(f32[1,192,64]{1,2,0:T(8,128)} %bitcast.167), channel_id=1, source_target_pairs={{0,1},{1,2},{2,3},{3,4},{4,5},{5,6},{6,7},{8,9},{9,10},{10,11},{11... | collective-permute-start | bytes 147464 | tf_op jit(solution)/shard_map/ppermute | solution.py:14
  116.7 9.6 %collective-permute-start.9 = (f32[1,192,120]{1,2,0:T(8,128)}, f32[1,192,120]{1,2,0:T(8,128)S(1)}, u32[]{:S(2)}, u32[]{:S(2)}) collective-permute-start(f32[1,192,120]{1,2,0:T(8,128)} %bitcast.169), channel_id=1, source_target_pairs={{128,0},{256,128},{384,256},{512,384},{640,512},{768,640},{896,768... | collective-permute-start | bytes 276488 | tf_op jit(solution)/shard_map/ppermute | solution.py:15
  118.0 8.4 %collective-permute-start.10 = (f32[1,192,120]{1,2,0:T(8,128)}, f32[1,192,120]{1,2,0:T(8,128)S(1)}, u32[]{:S(2)}, u32[]{:S(2)}) collective-permute-start(f32[1,192,120]{1,2,0:T(8,128)} %bitcast.168), channel_id=1, source_target_pairs={{8,0},{16,8},{24,16},{32,24},{40,32},{48,40},{56,48},{64,56},{72,6... | collective-permute-start | bytes 276488 | tf_op jit(solution)/shard_map/ppermute | solution.py:15
  119.9 14.2 %collective-permute-start.11 = (f32[1,192,64]{1,2,0:T(8,128)}, f32[1,192,64]{1,2,0:T(8,128)S(1)}, u32[]{:S(2)}, u32[]{:S(2)}) collective-permute-start(f32[1,192,64]{1,2,0:T(8,128)} %bitcast.165), channel_id=1, source_target_pairs={{1,0},{2,1},{3,2},{4,3},{5,4},{6,5},{7,6},{9,8},{10,9},{11,10},{12... | collective-permute-start | bytes 147464 | tf_op jit(solution)/shard_map/ppermute | solution.py:15
  238.2 16.7 %all-to-all-start.2 = ((f32[16,12,192]{2,1,0:T(8,128)}), f32[16,12,192]{2,1,0:T(8,128)S(1)}, u32[]{:S(2)}, u32[]{:S(2)}) async-start(f32[16,12,192]{2,1,0:T(8,128)} %broadcast_in_dim.29), calls=%async_computation.2 | async-start | bytes 524288 | tf_op jit(solution)/shard_map/all_to_all | solution.py:33
where the time goes:
time: 309 us; the launch traced here: 308 us
  blocking collectives  93.5 us (30%)
  other arithmetic  81.3 us (26%)
  starting transfers between devices  55.7 us (18%)
  local copies, waits for them, and re-layouts  39.6 us (13%)
  waiting for transfers between devices  32 us (10%)
  matrix products  3.7 us (1%)
    all_to_all x1, blocking collectives, from_everyone(): lax.all_to_all(jnp.broadcast_to(array[None], (size, *array.shape)), axis,...  70.9 us
    ppermute x6, starting transfers between devices, with_halo(): before = lax.ppermute(last, axis, up)  41.7 us
    another operation x7, other arithmetic, on_device(): lower = jnp.linalg.cholesky(correlation)  28.8 us
    all_to_all x1, blocking collectives, sum_at_owner(): lax.all_to_all(pieces, axis, split_axis=0, concat_axis=0, tiled=True)  22.6 us
    ppermute x6, waiting for transfers between devices, with_halo(): after = lax.ppermute(first, axis, down)  20.2 us
    another operation x6, other arithmetic, on_device(): jax.scipy.linalg.solve_triangular(lower, jnp.eye(width, dtype=jnp.float32...  19.8 us
    gather x12, local copies, waits for them, and re-layouts, pair(): return jnp.stack([values[:, low_list], values[:, up_list]])  16.1 us
    scatter-add x2, other arithmetic, apply(): total = cellsum.at[:, face_slots].add(received)  14.2 us
  transfers between devices with their start and end apart: 13, of which 4 were waited for; matrix products, arithmetic and copies ran while one was open for 7% of the time, Pallas kernels for 0%

commit v1 on v0

v1 whole, which is shorter than its diff:
```python
import functools
import jax
import jax.numpy as jnp
from jax import lax
from jax.experimental import pallas as pl
from jax.experimental.pallas import tpu as pltpu
from jax.sharding import PartitionSpec as P

MESH = pl.DeviceIdType.MESH
f32, bf16, i32 = jnp.float32, jnp.bfloat16, jnp.int32
WIDE = 1024
TILE = 512
HALF = 64


def half_tile(q):
    if q < 48:
        return 4 * q, 0
    return 128 + 4 * (q - 48), 128


def matmul(a, b, transposed=False):
    dims = (((1,), (1 if transposed else 0,)), ((), ()))
    return lax.dot_general(a, b, dims, preferred_element_type=f32)


def filter_kernel(
    sizes, table, conn, side, top, pidx, x_ref, k_ref, filt, gram,
    zeros, lists, inside, shift, xpad, rounded, cols, parts, cparts, pparts, zparts, csum, first, nodes, faces,
    snd_z, snd_p, rcv_z, rcv_p, part, got1, got2, got3, wide,
    hsend, hrecv, sends, recvs,
):
    ngx, ngy, ngz = sizes
    members, ring = ngy * (ngz // 2), 2 * ngx
    slots = x_ref.shape[1]
    corner = k_ref.shape[1]
    states = x_ref.shape[0]
    half = states // 2
    gx, gy, gz = lax.axis_index("gx"), lax.axis_index("gy"), lax.axis_index("gz")
    zhi, xq = lax.rem(gz, 2), gz // 2
    me = xq * ngy + gy
    zpos = zhi * ngx + gx
    here = {"gz": gz, "gx": gx, "gy": gy}

    def member(j):
        return {"gx": gx, "gy": lax.rem(j, ngy), "gz": (j // ngy) * 2 + zhi}

    def along_z(j):
        return {"gx": lax.rem(j, ngx), "gy": gy, "gz": xq * 2 + j // ngx}

    def step(axis, delta):
        return {**here, axis: here[axis] + delta}

    links = (("gz", -1, ngz), ("gz", 1, ngz), ("gx", -1, ngx), ("gx", 1, ngx), ("gy", -1, ngy), ("gy", 1, ngy))

    def exists(axis, delta, size):
        return here[axis] > 0 if delta < 0 else here[axis] < size - 1

    barrier = pltpu.get_barrier_semaphore()

    @pl.loop(1, members)
    def _(off):
        pl.semaphore_signal(barrier, inc=1, device_id=member(lax.rem(me + off, members)), device_id_type=MESH)

    @pl.loop(1, ring)
    def _(off):
        pl.semaphore_signal(barrier, inc=1, device_id=along_z(lax.rem(zpos + off, ring)), device_id_type=MESH)

    crosses = jnp.logical_or(jnp.logical_and(zhi == 1, gz < ngz - 1), jnp.logical_and(zhi == 0, gz > 0))

    @pl.when(crosses)
    def _():
        pl.semaphore_signal(barrier, inc=1, device_id=step("gz", 2 * zhi - 1), device_id_type=MESH)

    zeros[...] = jnp.zeros(zeros.shape, f32)
    lists[...] = jnp.full(lists.shape, -1, i32)
    lists[0:2, 0 : top.shape[1]] = top[...]
    lists[2:6, 0 : side.shape[1]] = side[...]
    plain = lists[...]
    rolled = pltpu.roll(plain, 64, 1)
    rows = [plain[0:1], plain[1:2], rolled[0:1], rolled[1:2], plain[2:3], plain[3:4], plain[4:5], plain[5:6]]
    chunk = 64

    @pl.loop(0, WIDE // chunk)
    def _(c):
        base = pl.multiple_of(c * chunk, chunk)
        level = lax.broadcasted_iota(i32, (chunk, 128), 0) + base
        for e in range(2):
            for b in range(corner // 128):
                col = e * corner + b * 128
                row = conn[e : e + 1, b * 128 : (b + 1) * 128]
                nodes[pl.ds(base, chunk), col : col + 128] = jnp.where(level == row, 1.0, 0.0).astype(bf16)
        for b, row in enumerate(rows):
            faces[pl.ds(base, chunk), b * 128 : (b + 1) * 128] = jnp.where(level == row, 1.0, 0.0).astype(bf16)

    inside[...] = jnp.full(inside.shape, -1, i32)
    inside[:, 0:slots] = pidx[...]
    index = inside[...]
    value = jnp.zeros((1, WIDE), f32)
    for t in range(table.shape[0]):
        value = jnp.where(index == t, table[t], value)
    shift[...] = value - 0.5
    xpad[:, WIDE - 128 : WIDE] = jnp.zeros((states, 128), bf16)
    xpad[:, 0:slots] = x_ref[...]

    def tiles(body):
        @pl.loop(0, WIDE // TILE)
        def _(n):
            body(pl.ds(pl.multiple_of(n * TILE, TILE), TILE))

    def put_split(ref, where, v):
        high = v.astype(bf16)
        ref[0 : v.shape[0], where] = high
        ref[v.shape[0] : 2 * v.shape[0], where] = (v - high.astype(f32)).astype(bf16)

    def joined(both):
        return both[: both.shape[0] // 2] + both[both.shape[0] // 2 :]

    def cell_sum(field):
        def gather(t):
            cols[:, t] = matmul(field[...], nodes[:, t]).astype(bf16)

        tiles(gather)

        @pl.loop(0, 2)
        def _(e):
            t = pl.ds(pl.multiple_of(e * corner, corner), corner)
            put_split(parts, t, matmul(cols[:, t], k_ref[e]))

        def scatter(t):
            v = joined(matmul(parts[...], nodes[t, :], True))
            csum[:, t] = v
            put_split(cparts, t, v)

        tiles(scatter)

    def exchange(a):
        zz = jnp.zeros((half, 256), f32)
        for h in range(2):
            for p in range(2):
                top_row = p * states + h * half
                zz = zz + matmul(cparts[top_row : top_row + half, :], faces[:, h * 256 : (h + 1) * 256])
        snd_z[a, 0] = zz[:, 0:128]
        snd_z[a, 1] = zz[:, 128:256]
        planes = joined(matmul(cparts[...], faces[:, 512:1024]))
        for d in range(4):
            snd_p[a, d] = planes[:, d * 128 : (d + 1) * 128]
        copies = []
        for d, link in enumerate(links):
            axis, delta, size = link
            src = snd_z.at[a, d] if d < 2 else snd_p.at[a, d - 2]
            dst = rcv_z.at[a, d ^ 1] if d < 2 else rcv_p.at[a, (d - 2) ^ 1]
            into = rcv_z.at[a, d] if d < 2 else rcv_p.at[a, d - 2]
            copy = pltpu.make_async_remote_copy(
                src_ref=src, dst_ref=dst, send_sem=hsend.at[a, d], recv_sem=hrecv.at[a, d ^ 1],
                device_id=step(axis, delta), device_id_type=MESH,
            )
            arrival = pltpu.make_async_remote_copy(
                src_ref=src, dst_ref=into, send_sem=hsend.at[a, d], recv_sem=hrecv.at[a, d],
                device_id=step(axis, delta), device_id_type=MESH,
            )
            there = exists(*link)

            @pl.when(there)
            def _():
                copy.start()

            @pl.when(jnp.logical_not(there))
            def _():
                empty = zeros.at[pl.ds(0, half)] if d < 2 else zeros
                pltpu.make_async_copy(empty, into, hrecv.at[a, d]).start()

            copies.append((there, copy, arrival))
        return copies

    def arrive(a, copies, finish):
        for _, _, arrival in copies:
            arrival.wait_recv()
        for d in range(4):
            put_split(pparts, slice(d * 128, (d + 1) * 128), rcv_p[a, d])
        for d in range(2):
            put_split(zparts, slice(d * 128, (d + 1) * 128), rcv_z[a, d])

        def add(t):
            planes = joined(matmul(pparts[...], faces[t, 512:1024], True))
            for h in range(2):
                zz = joined(matmul(zparts[...], faces[t, h * 256 : (h + 1) * 256], True))
                r = slice(h * half, (h + 1) * half)
                finish(r, t, csum[r, t] + planes[r] + zz)

        tiles(add)

    cell_sum(xpad)
    pl.semaphore_wait(barrier, members - 1 + ring - 1 + jnp.where(crosses, 1, 0))
    copies0 = exchange(0)

    def finish_first(r, t, total):
        v = (total + shift[:, t] * xpad[r, t].astype(f32)) / 3.0
        first[r, t] = v
        rounded[r, t] = v.astype(bf16)

    arrive(0, copies0, finish_first)
    cell_sum(rounded)
    copies1 = exchange(1)

    def finish_second(r, t, total):
        v = 2.0 * (total + shift[:, t] * first[r, t]) / 3.0 - xpad[r, t].astype(f32)
        rounded[r, t] = v.astype(bf16)

    arrive(1, copies1, finish_second)
    filt[...] = rounded[:, 0:slots]
    wide[:, 128:256] = jnp.zeros((states, 128), f32)
    wide[:, 0:states] = matmul(rounded[...], rounded[...], True)

    count = HALF // members
    for q in range(HALF):
        r, c = half_tile(q)
        part[q // count, q % count] = wide[r : r + 4, c : c + 128]
    got1[me] = part[me]

    @pl.loop(1, members)
    def _(off):
        j = lax.rem(me + off, members)
        pltpu.make_async_remote_copy(
            src_ref=part.at[j], dst_ref=got1.at[me], send_sem=sends.at[0], recv_sem=recvs.at[0],
            device_id=member(j), device_id_type=MESH,
        ).start()

    def all_of(ref, n, s):
        return pltpu.make_async_remote_copy(
            src_ref=ref.at[pl.ds(0, n)], dst_ref=ref.at[pl.ds(0, n)], send_sem=sends.at[s], recv_sem=recvs.at[s],
            device_id=along_z(lax.rem(zpos + 1, ring)), device_id_type=MESH,
        )

    all_of(got1, members - 1, 0).wait_recv()
    got2[zpos] = jnp.sum(got1[...], axis=0)

    @pl.loop(1, ring)
    def _(off):
        pltpu.make_async_remote_copy(
            src_ref=got2.at[zpos], dst_ref=got2.at[zpos], send_sem=sends.at[1], recv_sem=recvs.at[1],
            device_id=along_z(lax.rem(zpos + off, ring)), device_id_type=MESH,
        ).start()

    all_of(got2, ring - 1, 1).wait_recv()
    got3[me] = jnp.sum(got2[...], axis=0)

    @pl.loop(1, members)
    def _(off):
        pltpu.make_async_remote_copy(
            src_ref=got3.at[me], dst_ref=got3.at[me], send_sem=sends.at[2], recv_sem=recvs.at[2],
            device_id=member(lax.rem(me + off, members)), device_id_type=MESH,
        ).start()

    all_of(got3, members - 1, 2).wait_recv()
    gram[0:128, 128:256] = jnp.zeros((128, 128), f32)
    for q in range(HALF):
        r, c = half_tile(q)
        gram[r : r + 4, c : c + 128] = got3[q // count, q % count]
    for there, copy, _ in copies0 + copies1:

        @pl.when(there)
        def _():
            copy.wait_send()

    all_of(got1, members - 1, 0).wait_send()
    all_of(got2, ring - 1, 1).wait_send()
    all_of(got3, members - 1, 2).wait_send()


def filtered_gram(sizes, table, conn, side, top, pidx, x, k):
    ngx, ngy, ngz = sizes
    members, ring = ngy * (ngz // 2), 2 * ngx
    count = HALF // members
    states, slots = x.shape
    whole = pl.BlockSpec(memory_space=pltpu.VMEM)
    halves = (count, 4, 128)
    return pl.pallas_call(
        functools.partial(filter_kernel, sizes),
        out_shape=(jax.ShapeDtypeStruct(x.shape, bf16), jax.ShapeDtypeStruct((states, 256), f32)),
        in_specs=[pl.BlockSpec(memory_space=pltpu.SMEM)] + [whole] * 6,
        out_specs=(whole, whole),
        scratch_shapes=[
            pltpu.VMEM((states, 128), f32),
            pltpu.VMEM((8, 128), i32),
            pltpu.VMEM((1, WIDE), i32),
            pltpu.VMEM((1, WIDE), f32),
            pltpu.VMEM((states, WIDE), bf16),
            pltpu.VMEM((states, WIDE), bf16),
            pltpu.VMEM((states, WIDE), bf16),
            pltpu.VMEM((2 * states, WIDE), bf16),
            pltpu.VMEM((2 * states, WIDE), bf16),
            pltpu.VMEM((2 * states, 512), bf16),
            pltpu.VMEM((states, 256), bf16),
            pltpu.VMEM((states, WIDE), f32),
            pltpu.VMEM((states, WIDE), f32),
            pltpu.VMEM((WIDE, 1024), bf16),
            pltpu.VMEM((WIDE, 1024), bf16),
            pltpu.VMEM((2, 2, states // 2, 128), f32),
            pltpu.VMEM((2, 4, states, 128), f32),
            pltpu.VMEM((2, 2, states // 2, 128), f32),
            pltpu.VMEM((2, 4, states, 128), f32),
            pltpu.VMEM((members, *halves), f32),
            pltpu.VMEM((members, *halves), f32),
            pltpu.VMEM((ring, *halves), f32),
            pltpu.VMEM((members, *halves), f32),
            pltpu.VMEM((states, 256), f32),
            pltpu.SemaphoreType.DMA((2, 6)),
            pltpu.SemaphoreType.DMA((2, 6)),
            pltpu.SemaphoreType.DMA((3,)),
            pltpu.SemaphoreType.DMA((3,)),
        ],
        compiler_params=pltpu.CompilerParams(collective_id=0, has_side_effects=True, vmem_limit_bytes=56 << 20),
        name="filter_gram",
    )(table, conn, side, top, pidx, x, k)


def eliminate(a_ref, states):
    groups = states // 8
    lane = lax.broadcasted_iota(i32, (1, 256), 1)
    sub = lax.broadcasted_iota(i32, (8, 1), 0)
    a = [a_ref[8 * g : 8 * g + 8, :] for g in range(groups)]
    for g in range(groups):
        for t in range(8):
            k = 8 * g + t
            row = a[g][t : t + 1, :]
            scaled = (row + jnp.where(lane == k, 1.0, 0.0)) * (1.0 / row[:, k : k + 1])
            for h in range(g + 1, groups):
                a[h] = a[h] - a[h][:, k : k + 1] * scaled
            a[g] = a[g] - jnp.where(sub > t, a[g][:, k : k + 1], 0.0) * scaled
        a_ref[8 * g : 8 * g + 8, :] = a[g]


def rotate_kernel(total_slots, gram, filt, out, work):
    states = filt.shape[0]
    work[...] = gram[...] * (1.0 / total_slots)
    work[0:128, 128:states] = work[128:states, 0:128].T
    full = work[...]
    row = lax.broadcasted_iota(i32, full.shape, 0)
    col = lax.broadcasted_iota(i32, full.shape, 1)
    diag = jnp.where(row == col, full, 0.0)
    across = jnp.sum(diag, axis=0, keepdims=True)
    across = lax.rsqrt(jnp.where(col[0:1] < states, across, 1.0))
    down = lax.rsqrt(jnp.sum(diag, axis=1, keepdims=True))
    work[...] = full * across * down
    eliminate(work, states)
    done = work[...]
    pivot = jnp.sum(jnp.where(row == col, done, 0.0), axis=1, keepdims=True)
    lower = jnp.where(col < row, done, jnp.where(col == row, 1.0, 0.0))
    inverse = (lower * lax.rsqrt(pivot) * across)[:, :states].astype(bf16)
    out[...] = matmul(inverse, filt[...]).astype(bf16)


def rotated(total_slots, gram, filt):
    whole = pl.BlockSpec(memory_space=pltpu.VMEM)
    return pl.pallas_call(
        functools.partial(rotate_kernel, total_slots),
        out_shape=jax.ShapeDtypeStruct(filt.shape, bf16),
        in_specs=[whole] * 2,
        out_specs=whole,
        scratch_shapes=[pltpu.VMEM(gram.shape, f32)],
        name="rotate",
    )(gram, filt)


def on_device(sizes, states, cell_matrices, connectivity, side_nodes, top_nodes, pot_index, pot_table):
    filt, gram = filtered_gram(
        sizes, pot_table, connectivity, side_nodes, top_nodes, pot_index[None, :], states, cell_matrices
    )
    total_slots = states.shape[1] * sizes[0] * sizes[1] * sizes[2]
    return rotated(total_slots, gram, filt)


def solution(mesh):
    sizes = tuple(mesh.shape[name] for name in ("gx", "gy", "gz"))
    in_specs = (
        P(None, ("gx", "gy", "gz")),
        P(("gx", "gy", "gz"), None, None),
        P(("gx", "gy", "gz"), None),
        P(None, ("gx", "gy", "gz")),
        P(None, ("gx", "gy", "gz")),
        P(("gx", "gy", "gz")),
        P(),
    )
    out_specs = P(None, ("gx", "gy", "gz"))
    return jax.shard_map(
        functools.partial(on_device, sizes), mesh=mesh, in_specs=in_specs, out_specs=out_specs, check_vma=False
    )
```

time: 309 us -> 100 us (0.32)
  Pallas kernels: 0 us -> 100 us
  blocking collectives: 93.5 us -> 0 us
  other arithmetic: 81.3 us -> 0 us
  starting transfers between devices: 55.7 us -> 0 us
  local copies, waits for them, and re-layouts: 39.6 us -> 0 us
  waiting for transfers between devices: 32 us -> 0 us
  matrix products: 3.7 us -> 0 us
    pallas_call x0 -> x2, Pallas kernels: none -> 100 us  [the longest x1 81.6 us: filtered_gram(): pl.pallas_call(functools.partial(filter_kernel, sizes), out_shape=(jax.Sh...]
    all_to_all x2 -> x0, blocking collectives: 93.5 us -> none  [the longest x1 70.9 us: from_everyone(): lax.all_to_all(jnp.broadcast_to(array[None], (size, *array.shape)), axis,...]
    ppermute x12 -> x0, starting transfers between devices: 50.8 us -> none  [the longest x6 41.7 us: with_halo(): before = lax.ppermute(last, axis, up)]
    another operation x15 -> x0, other arithmetic: 50 us -> none  [the longest x7 28.8 us: on_device(): lower = jnp.linalg.cholesky(correlation)]
    scatter-add x4 -> x0, other arithmetic: 27.8 us -> none  [the longest x2 14.2 us: apply(): total = cellsum.at[:, face_slots].add(received)]
    gather x14 -> x0, local copies, waits for them, and re-layouts: 25 us -> none  [the longest x12 16.1 us: pair(): return jnp.stack([values[:, low_list], values[:, up_list]])]
    ppermute x12 -> x0, waiting for transfers between devices: 20.3 us -> none  [the longest x6 20.2 us: with_halo(): after = lax.ppermute(first, axis, down)]
    all_to_all x1 -> x0, waiting for transfers between devices: 11.7 us -> none  [from_everyone(): lax.all_to_all(jnp.broadcast_to(array[None], (size, *array.shape)), axis,...]
  transfers between devices with their start and end apart: 13 -> 0, of which waited for: 4 -> 0; matrix products, arithmetic and copies ran while one was open for 7% -> 0% of each run, Pallas kernels for 0% -> 0%
where the time goes in v1:
time: 100 us
  Pallas kernels  100 us (100%)
    pallas_call x1, Pallas kernels, filtered_gram(): pl.pallas_call(functools.partial(filter_kernel, sizes), out_shape=(jax.Sh...  81.6 us
    pallas_call x1, Pallas kernels, rotated(): pl.pallas_call(functools.partial(rotate_kernel, total_slots), out_shape=j...  18.6 us

profile of v1, /device:TPU:1, one launch (start us, length us, event | category | flops | bytes accessed | tf_op | source)
XLA Modules:
  0.0 100.2 jit_solution(17851368275076763936)
XLA Ops:
  0.0 81.6 %filter_gram.1 = (bf16[192,960]{1,0:T(8,128)(2,1)}, f32[192,256]{1,0:T(8,128)}) custom-call(f32[64]{0:T(128)} %table.1, s32[2,512]{1,0:T(2,128)} %conn.1, s32[4,120]{1,0:T(4,128)} %side.1, s32[2,64]{1,0:T(2,128)} %top.1, s32[1,960]{1,0:T(1,128)} %bitcast.1, bf16[192,960]{1,0:T(8,128)(2,1)} %x_ref.1, bf16[2,512,512]{2,1,0:T(8,128)(2,1)} %k_ref.1), custom_call_target="tpu_custom_call" | custom-call | tf_op jit(solution)/shard_map/filter_gram/pallas_call | solution.py:278
  81.6 18.6 %rotate.1 = bf16[192,960]{1,0:T(8,128)(2,1)} custom-call(f32[192,256]{1,0:T(8,128)} %get-tuple-element.7.gram, bf16[192,960]{1,0:T(8,128)(2,1)} %get-tuple-element.8.filt), custom_call_target="tpu_custom_call" | custom-call | tf_op jit(solution)/shard_map/rotate/pallas_call | solution.py:356

commit v2 on v1

--- a/solution.py
+++ b/solution.py
@@ -26,7 +26,7 @@
 
 def filter_kernel(
     sizes, table, conn, side, top, pidx, x_ref, k_ref, filt, gram,
-    zeros, lists, inside, shift, xpad, rounded, cols, parts, cparts, pparts, zparts, csum, first, nodes, faces,
+    zeros, lists, inside, shift, xpad, rounded, cols, parts, cparts, pparts, zparts, csum, first, nodes, faces, cellmat, facemat,
     snd_z, snd_p, rcv_z, rcv_p, part, got1, got2, got3, wide,
     hsend, hrecv, sends, recvs,
 ):
@@ -42,11 +42,28 @@
     zpos = zhi * ngx + gx
     here = {"gz": gz, "gx": gx, "gy": gy}
 
-    def member(j):
-        return {"gx": gx, "gy": lax.rem(j, ngy), "gz": (j // ngy) * 2 + zhi}
-
-    def along_z(j):
-        return {"gx": lax.rem(j, ngx), "gy": gy, "gz": xq * 2 + j // ngx}
+    def wrap(v, n):
+        return jnp.where(v >= n, v - n, v)
+
+    def far_first(i, n):
+        even = lax.rem(i, 2) == 0
+        return n // 2 + jnp.where(even, i // 2, -((i + 1) // 2))
+
+    def over_plane(body):
+        for ox in sorted(range(ngz // 2), key=lambda v: -min(v, ngz // 2 - v)):
+            x = wrap(xq + ox, ngz // 2)
+
+            @pl.loop(0, ngy if ox else ngy - 1)
+            def _(i):
+                y = wrap(gy + far_first(i, ngy), ngy)
+                body(x * ngy + y, {"gx": gx, "gy": y, "gz": 2 * x + zhi})
+
+    def over_ring(body):
+        @pl.loop(0, ring - 1)
+        def _(i):
+            z = wrap(zpos + far_first(i, ring), ring)
+            high = jnp.where(z >= ngx, 1, 0)
+            body({"gx": z - high * ngx, "gy": gy, "gz": 2 * xq + high})
 
     def step(axis, delta):
         return {**here, axis: here[axis] + delta}
@@ -58,19 +75,17 @@
 
     barrier = pltpu.get_barrier_semaphore()
 
-    @pl.loop(1, members)
-    def _(off):
-        pl.semaphore_signal(barrier, inc=1, device_id=member(lax.rem(me + off, members)), device_id_type=MESH)
-
-    @pl.loop(1, ring)
-    def _(off):
-        pl.semaphore_signal(barrier, inc=1, device_id=along_z(lax.rem(zpos + off, ring)), device_id_type=MESH)
+    def greet(place):
+        pl.semaphore_signal(barrier, inc=1, device_id=place, device_id_type=MESH)
 
     crosses = jnp.logical_or(jnp.logical_and(zhi == 1, gz < ngz - 1), jnp.logical_and(zhi == 0, gz > 0))
 
     @pl.when(crosses)
     def _():
-        pl.semaphore_signal(barrier, inc=1, device_id=step("gz", 2 * zhi - 1), device_id_type=MESH)
+        greet(step("gz", 2 * zhi - 1))
+
+    over_ring(greet)
+    over_plane(lambda j, place: greet(place))
 
     zeros[...] = jnp.zeros(zeros.shape, f32)
     lists[...] = jnp.full(lists.shape, -1, i32)
@@ -134,82 +149,120 @@
 
         tiles(scatter)
 
-    def exchange(a):
-        zz = jnp.zeros((half, 256), f32)
-        for h in range(2):
-            for p in range(2):
-                top_row = p * states + h * half
-                zz = zz + matmul(cparts[top_row : top_row + half, :], faces[:, h * 256 : (h + 1) * 256])
-        snd_z[a, 0] = zz[:, 0:128]
-        snd_z[a, 1] = zz[:, 128:256]
-        planes = joined(matmul(cparts[...], faces[:, 512:1024]))
-        for d in range(4):
-            snd_p[a, d] = planes[:, d * 128 : (d + 1) * 128]
-        copies = []
-        for d, link in enumerate(links):
-            axis, delta, size = link
-            src = snd_z.at[a, d] if d < 2 else snd_p.at[a, d - 2]
-            dst = rcv_z.at[a, d ^ 1] if d < 2 else rcv_p.at[a, (d - 2) ^ 1]
-            into = rcv_z.at[a, d] if d < 2 else rcv_p.at[a, d - 2]
-            copy = pltpu.make_async_remote_copy(
-                src_ref=src, dst_ref=dst, send_sem=hsend.at[a, d], recv_sem=hrecv.at[a, d ^ 1],
-                device_id=step(axis, delta), device_id_type=MESH,
-            )
-            arrival = pltpu.make_async_remote_copy(
-                src_ref=src, dst_ref=into, send_sem=hsend.at[a, d], recv_sem=hrecv.at[a, d],
-                device_id=step(axis, delta), device_id_type=MESH,
-            )
-            there = exists(*link)
+    def landing(a, d):
+        return rcv_z.at[a, d] if d < 2 else rcv_p.at[a, d - 2]
+
+    def outgoing(a, d):
+        axis, delta, size = links[d]
+        return pltpu.make_async_remote_copy(
+            src_ref=snd_z.at[a, d] if d < 2 else snd_p.at[a, d - 2], dst_ref=landing(a, d ^ 1),
+            send_sem=hsend.at[a, d], recv_sem=hrecv.at[a, d ^ 1],
+            device_id=step(axis, delta), device_id_type=MESH,
+        )
+
+    def incoming(a, d):
+        axis, delta, size = links[d]
+        return pltpu.make_async_remote_copy(
+            src_ref=landing(a, d), dst_ref=landing(a, d), send_sem=hsend.at[a, d], recv_sem=hrecv.at[a, d],
+            device_id=step(axis, delta), device_id_type=MESH,
+        )
+
+    def send(a, which):
+        for d in which:
+            there = exists(*links[d])
 
             @pl.when(there)
             def _():
-                copy.start()
+                outgoing(a, d).start()
 
             @pl.when(jnp.logical_not(there))
             def _():
                 empty = zeros.at[pl.ds(0, half)] if d < 2 else zeros
-                pltpu.make_async_copy(empty, into, hrecv.at[a, d]).start()
-
-            copies.append((there, copy, arrival))
-        return copies
-
-    def arrive(a, copies, finish):
-        for _, _, arrival in copies:
-            arrival.wait_recv()
+                pltpu.make_async_copy(empty, landing(a, d), hrecv.at[a, d]).start()
+
+    def store_z(a, zz):
+        snd_z[a, 0] = zz[:, 0:128]
+        snd_z[a, 1] = zz[:, 128:256]
+
+    def store_planes(a, planes):
+        for d in range(4):
+            snd_p[a, d] = planes[:, d * 128 : (d + 1) * 128]
+
+    def arrive(a, finish):
+        for d in range(2, 6):
+            incoming(a, d).wait_recv()
         for d in range(4):
             put_split(pparts, slice(d * 128, (d + 1) * 128), rcv_p[a, d])
+
+        def add_planes(t):
+            csum[:, t] = csum[:, t] + joined(matmul(pparts[...], faces[t, 512:1024], True))
+
+        tiles(add_planes)
+        for d in range(2):
+            incoming(a, d).wait_recv()
         for d in range(2):
             put_split(zparts, slice(d * 128, (d + 1) * 128), rcv_z[a, d])
 
-        def add(t):
-            planes = joined(matmul(pparts[...], faces[t, 512:1024], True))
+        def add_z(t):
             for h in range(2):
                 zz = joined(matmul(zparts[...], faces[t, h * 256 : (h + 1) * 256], True))
                 r = slice(h * half, (h + 1) * half)
-                finish(r, t, csum[r, t] + planes[r] + zz)
-
-        tiles(add)
+                finish(r, t, csum[r, t] + zz)
+
+        tiles(add_z)
 
     cell_sum(xpad)
+    zz = jnp.zeros((half, 256), f32)
+    for h in range(2):
+        for p in range(2):
+            top_row = p * states + h * half
+            zz = zz + matmul(cparts[top_row : top_row + half, :], faces[:, h * 256 : (h + 1) * 256])
+    store_z(0, zz)
+    store_planes(0, joined(matmul(cparts[...], faces[:, 512:1024])))
     pl.semaphore_wait(barrier, members - 1 + ring - 1 + jnp.where(crosses, 1, 0))
-    copies0 = exchange(0)
+    send(0, range(6))
+
+    @pl.loop(0, 2)
+    def _(e):
+        c = pl.ds(pl.multiple_of(e * corner, corner), corner)
+
+        def spread_cell(t):
+            cellmat[c, t] = matmul(k_ref[e], nodes[t, c], True).astype(bf16)
+
+        tiles(spread_cell)
+
+        def spread_faces(t):
+            facemat[c, t] = matmul(cellmat[c, :], faces[:, t]).astype(bf16)
+
+        tiles(spread_faces)
 
     def finish_first(r, t, total):
         v = (total + shift[:, t] * xpad[r, t].astype(f32)) / 3.0
         first[r, t] = v
         rounded[r, t] = v.astype(bf16)
 
-    arrive(0, copies0, finish_first)
-    cell_sum(rounded)
-    copies1 = exchange(1)
+    arrive(0, finish_first)
+
+    def gather_second(t):
+        cols[:, t] = matmul(rounded[...], nodes[:, t]).astype(bf16)
+
+    tiles(gather_second)
+    store_z(1, matmul(cols[0:half, :], facemat[:, 0:256]) + matmul(cols[half:states, :], facemat[:, 256:512]))
+    send(1, range(2))
+    store_planes(1, matmul(cols[...], facemat[:, 512:1024]))
+    send(1, range(2, 6))
+
+    def second_sum(t):
+        csum[:, t] = matmul(cols[...], cellmat[:, t])
+
+    tiles(second_sum)
 
     def finish_second(r, t, total):
         v = 2.0 * (total + shift[:, t] * first[r, t]) / 3.0 - xpad[r, t].astype(f32)
         rounded[r, t] = v.astype(bf16)
 
-    arrive(1, copies1, finish_second)
-    filt[...] = rounded[:, 0:slots]
     wide[:, 128:256] = jnp.zeros((states, 128), f32)
+    arrive(1, finish_second)
     wide[:, 0:states] = matmul(rounded[...], rounded[...], True)
 
     count = HALF // members
@@ -218,50 +271,52 @@
         part[q // count, q % count] = wide[r : r + 4, c : c + 128]
     got1[me] = part[me]
 
-    @pl.loop(1, members)
-    def _(off):
-        j = lax.rem(me + off, members)
+    def scatter(j, place):
         pltpu.make_async_remote_copy(
             src_ref=part.at[j], dst_ref=got1.at[me], send_sem=sends.at[0], recv_sem=recvs.at[0],
-            device_id=member(j), device_id_type=MESH,
+            device_id=place, device_id_type=MESH,
         ).start()
+
+    over_plane(scatter)
+    filt[...] = rounded[:, 0:slots]
+    gram[0:128, 128:256] = jnp.zeros((128, 128), f32)
 
     def all_of(ref, n, s):
         return pltpu.make_async_remote_copy(
             src_ref=ref.at[pl.ds(0, n)], dst_ref=ref.at[pl.ds(0, n)], send_sem=sends.at[s], recv_sem=recvs.at[s],
-            device_id=along_z(lax.rem(zpos + 1, ring)), device_id_type=MESH,
+            device_id={**here, "gy": wrap(gy + 1, ngy)}, device_id_type=MESH,
         )
 
     all_of(got1, members - 1, 0).wait_recv()
     got2[zpos] = jnp.sum(got1[...], axis=0)
 
-    @pl.loop(1, ring)
-    def _(off):
+    def along(place):
         pltpu.make_async_remote_copy(
             src_ref=got2.at[zpos], dst_ref=got2.at[zpos], send_sem=sends.at[1], recv_sem=recvs.at[1],
-            device_id=along_z(lax.rem(zpos + off, ring)), device_id_type=MESH,
+            device_id=place, device_id_type=MESH,
         ).start()
 
+    over_ring(along)
     all_of(got2, ring - 1, 1).wait_recv()
     got3[me] = jnp.sum(got2[...], axis=0)
 
-    @pl.loop(1, members)
-    def _(off):
+    def gather_all(j, place):
         pltpu.make_async_remote_copy(
             src_ref=got3.at[me], dst_ref=got3.at[me], send_sem=sends.at[2], recv_sem=recvs.at[2],
-            device_id=member(lax.rem(me + off, members)), device_id_type=MESH,
+            device_id=place, device_id_type=MESH,
         ).start()
 
+    over_plane(gather_all)
     all_of(got3, members - 1, 2).wait_recv()
-    gram[0:128, 128:256] = jnp.zeros((128, 128), f32)
     for q in range(HALF):
         r, c = half_tile(q)
         gram[r : r + 4, c : c + 128] = got3[q // count, q % count]
-    for there, copy, _ in copies0 + copies1:
-
-        @pl.when(there)
-        def _():
-            copy.wait_send()
+    for a in range(2):
+        for d in range(6):
+
+            @pl.when(exists(*links[d]))
+            def _():
+                outgoing(a, d).wait_send()
 
     all_of(got1, members - 1, 0).wait_send()
     all_of(got2, ring - 1, 1).wait_send()
@@ -296,6 +351,8 @@
             pltpu.VMEM((states, WIDE), f32),
             pltpu.VMEM((WIDE, 1024), bf16),
             pltpu.VMEM((WIDE, 1024), bf16),
+            pltpu.VMEM((WIDE, 1024), bf16),
+            pltpu.VMEM((WIDE, 1024), bf16),
             pltpu.VMEM((2, 2, states // 2, 128), f32),
             pltpu.VMEM((2, 4, states, 128), f32),
             pltpu.VMEM((2, 2, states // 2, 128), f32),
@@ -317,18 +374,58 @@
 
 def eliminate(a_ref, states):
     groups = states // 8
-    lane = lax.broadcasted_iota(i32, (1, 256), 1)
-    sub = lax.broadcasted_iota(i32, (8, 1), 0)
-    a = [a_ref[8 * g : 8 * g + 8, :] for g in range(groups)]
-    for g in range(groups):
-        for t in range(8):
-            k = 8 * g + t
-            row = a[g][t : t + 1, :]
-            scaled = (row + jnp.where(lane == k, 1.0, 0.0)) * (1.0 / row[:, k : k + 1])
-            for h in range(g + 1, groups):
-                a[h] = a[h] - a[h][:, k : k + 1] * scaled
-            a[g] = a[g] - jnp.where(sub > t, a[g][:, k : k + 1], 0.0) * scaled
-        a_ref[8 * g : 8 * g + 8, :] = a[g]
+    lane = lax.broadcasted_iota(i32, (8, 256), 1)
+    sub = lax.broadcasted_iota(i32, (8, 256), 0)
+    sub1 = sub[:, 0:128]
+
+    def spread(v, k):
+        return jnp.broadcast_to(v[:, k : k + 1], (8, 128))
+
+    def twice(v):
+        return jnp.concatenate([v, v], axis=1)
+
+    def pivots(g, r):
+        first = 8 * g
+        c = [spread(r, first + t) for t in range(8)]
+        keep = r
+        scale = jnp.zeros((8, 128), f32)
+        def full(v):
+            return jnp.broadcast_to(v, (8, 128))
+
+        for t in range(0, 8, 2):
+            p, q, s = full(c[t][t : t + 1]), full(c[t + 1][t : t + 1]), full(c[t + 1][t + 1 : t + 2])
+            one = 1.0 / p
+            two = p * (1.0 / (p * s - q * q))
+            m = jnp.where(sub1 == t, 0.0, c[t] * one)
+            n = jnp.where(sub1 == t + 1, 0.0, (c[t + 1] - m * q) * two)
+            for u in range(t + 2, 8):
+                v = c[u] - m * c[u][t : t + 1]
+                c[u] = v - n * v[t + 1 : t + 2]
+            for k, inv, mult in ((t, one, m), (t + 1, two, n)):
+                row = r[k : k + 1]
+                keep = jnp.where(sub == k, row, keep)
+                scale = jnp.where(sub1 == k, inv, scale)
+                unit = jnp.where(lane[0:1] == first + k, 1.0, row)
+                r = jnp.where(lane == first + k, jnp.where(sub == k, 1.0, 0.0), r) - twice(mult) * unit
+        a_ref[first : first + 8, :] = keep
+        return r * twice(scale)
+
+    def update(g, r, v):
+        first = 8 * g
+        inside = jnp.logical_and(lane >= first, lane < first + 8)
+        terms = [twice(spread(v, first + t)) * r[t : t + 1] for t in range(8)]
+        while len(terms) > 1:
+            terms = [terms[i] + terms[i + 1] for i in range(0, len(terms), 2)]
+        return jnp.where(inside, 0.0, v) - terms[0]
+
+    r = pivots(0, a_ref[0:8, :])
+    for g in range(groups - 1):
+        nxt = slice(8 * g + 8, 8 * g + 16)
+        ahead = pivots(g + 1, update(g, r, a_ref[nxt, :]))
+        for h in range(g + 2, groups):
+            rows = slice(8 * h, 8 * h + 8)
+            a_ref[rows, :] = update(g, r, a_ref[rows, :])
+        r = ahead
 
 
 def rotate_kernel(total_slots, gram, filt, out, work):

time: 100 us -> 85.4 us (0.85)
  Pallas kernels: 100 us -> 85.2 us
    pallas_call x1, Pallas kernels: 18.6 us -> 8.92 us  [rotated(): pl.pallas_call(functools.partial(rotate_kernel, total_slots), out_shape=j...]
    pallas_call x1, Pallas kernels: 81.6 us -> 76.3 us  [filtered_gram(): pl.pallas_call(functools.partial(filter_kernel, sizes), out_shape=(jax.Sh...]
where the time goes in v2:
time: 85.4 us; the launch traced here: 85.2 us
  Pallas kernels  85.2 us (100%)
    pallas_call x1, Pallas kernels, filtered_gram(): pl.pallas_call(functools.partial(filter_kernel, sizes), out_shape=(jax.Sh...  76.3 us
    pallas_call x1, Pallas kernels, rotated(): pl.pallas_call(functools.partial(rotate_kernel, total_slots), out_shape=j...  8.92 us

profile of v2, /device:TPU:1, one launch (start us, length us, event | category | flops | bytes accessed | tf_op | source)
XLA Modules:
  0.0 85.2 jit_solution(4894573396864417453)
XLA Ops:
  0.0 76.3 %filter_gram.1 = (bf16[192,960]{1,0:T(8,128)(2,1)}, f32[192,256]{1,0:T(8,128)}) custom-call(f32[64]{0:T(128)} %table.1, s32[2,512]{1,0:T(2,128)} %conn.1, s32[4,120]{1,0:T(4,128)} %side.1, s32[2,64]{1,0:T(2,128)} %top.1, s32[1,960]{1,0:T(1,128)} %bitcast.1, bf16[192,960]{1,0:T(8,128)(2,1)} %x_ref.1, bf16[2,512,512]{2,1,0:T(8,128)(2,1)} %k_ref.1), custom_call_target="tpu_custom_call" | custom-call | tf_op jit(solution)/shard_map/filter_gram/pallas_call | solution.py:333
  76.3 8.9 %rotate.1 = bf16[192,960]{1,0:T(8,128)(2,1)} custom-call(f32[192,256]{1,0:T(8,128)} %get-tuple-element.7.gram, bf16[192,960]{1,0:T(8,128)(2,1)} %get-tuple-element.8.filt), custom_call_target="tpu_custom_call" | custom-call | tf_op jit(solution)/shard_map/rotate/pallas_call | solution.py:453

commit v3 on v2

--- a/solution.py
+++ b/solution.py
@@ -25,12 +25,17 @@
 
 
 def filter_kernel(
-    sizes, table, conn, side, top, pidx, x_ref, k_ref, filt, gram,
+    sizes, table, conn, side, top, pidx, x_hbm, k_hbm, filt, gram,
     zeros, lists, inside, shift, xpad, rounded, cols, parts, cparts, pparts, zparts, csum, first, nodes, faces, cellmat, facemat,
     snd_z, snd_p, rcv_z, rcv_p, part, got1, got2, got3, wide,
-    hsend, hrecv, sends, recvs,
+    x_ref, k_ref, fbuf, hsend, hrecv, sends, recvs, loads,
 ):
     ngx, ngy, ngz = sizes
+    load_x = pltpu.make_async_copy(x_hbm, x_ref, loads.at[0])
+    load_k = pltpu.make_async_copy(k_hbm, k_ref, loads.at[1])
+    store_f = pltpu.make_async_copy(fbuf, filt, loads.at[2])
+    load_x.start()
+    load_k.start()
     members, ring = ngy * (ngz // 2), 2 * ngx
     slots = x_ref.shape[1]
     corner = k_ref.shape[1]
@@ -116,6 +121,7 @@
         value = jnp.where(index == t, table[t], value)
     shift[...] = value - 0.5
     xpad[:, WIDE - 128 : WIDE] = jnp.zeros((states, 128), bf16)
+    load_x.wait()
     xpad[:, 0:slots] = x_ref[...]
 
     def tiles(body):
@@ -131,11 +137,12 @@
     def joined(both):
         return both[: both.shape[0] // 2] + both[both.shape[0] // 2 :]
 
-    def cell_sum(field):
+    def first_sum(field):
         def gather(t):
             cols[:, t] = matmul(field[...], nodes[:, t]).astype(bf16)
 
         tiles(gather)
+        load_k.wait()
 
         @pl.loop(0, 2)
         def _(e):
@@ -211,16 +218,17 @@
 
         tiles(add_z)
 
-    cell_sum(xpad)
+    first_sum(xpad)
     zz = jnp.zeros((half, 256), f32)
     for h in range(2):
         for p in range(2):
             top_row = p * states + h * half
             zz = zz + matmul(cparts[top_row : top_row + half, :], faces[:, h * 256 : (h + 1) * 256])
     store_z(0, zz)
+    pl.semaphore_wait(barrier, members - 1 + ring - 1 + jnp.where(crosses, 1, 0))
+    send(0, range(2))
     store_planes(0, joined(matmul(cparts[...], faces[:, 512:1024])))
-    pl.semaphore_wait(barrier, members - 1 + ring - 1 + jnp.where(crosses, 1, 0))
-    send(0, range(6))
+    send(0, range(2, 6))
 
     @pl.loop(0, 2)
     def _(e):
@@ -278,7 +286,8 @@
         ).start()
 
     over_plane(scatter)
-    filt[...] = rounded[:, 0:slots]
+    fbuf[...] = rounded[:, 0:slots]
+    store_f.start()
     gram[0:128, 128:256] = jnp.zeros((128, 128), f32)
 
     def all_of(ref, n, s):
@@ -318,6 +327,7 @@
             def _():
                 outgoing(a, d).wait_send()
 
+    store_f.wait()
     all_of(got1, members - 1, 0).wait_send()
     all_of(got2, ring - 1, 1).wait_send()
     all_of(got3, members - 1, 2).wait_send()
@@ -329,12 +339,13 @@
     count = HALF // members
     states, slots = x.shape
     whole = pl.BlockSpec(memory_space=pltpu.VMEM)
+    far = pl.BlockSpec(memory_space=pl.ANY)
     halves = (count, 4, 128)
     return pl.pallas_call(
         functools.partial(filter_kernel, sizes),
         out_shape=(jax.ShapeDtypeStruct(x.shape, bf16), jax.ShapeDtypeStruct((states, 256), f32)),
-        in_specs=[pl.BlockSpec(memory_space=pltpu.SMEM)] + [whole] * 6,
-        out_specs=(whole, whole),
+        in_specs=[pl.BlockSpec(memory_space=pltpu.SMEM)] + [whole] * 4 + [far] * 2,
+        out_specs=(far, whole),
         scratch_shapes=[
             pltpu.VMEM((states, 128), f32),
             pltpu.VMEM((8, 128), i32),
@@ -362,8 +373,12 @@
             pltpu.VMEM((ring, *halves), f32),
             pltpu.VMEM((members, *halves), f32),
             pltpu.VMEM((states, 256), f32),
+            pltpu.VMEM(x.shape, bf16),
+            pltpu.VMEM(k.shape, bf16),
+            pltpu.VMEM(x.shape, bf16),
             pltpu.SemaphoreType.DMA((2, 6)),
             pltpu.SemaphoreType.DMA((2, 6)),
+            pltpu.SemaphoreType.DMA((3,)),
             pltpu.SemaphoreType.DMA((3,)),
             pltpu.SemaphoreType.DMA((3,)),
         ],

time: 85.4 us -> 84.7 us (level)
  no operation moved by 1% of the time
where the time goes in v3:
time: 84.7 us; the launch traced here: 84.6 us
  Pallas kernels  84.5 us (100%)
    pallas_call x1, Pallas kernels, filtered_gram(): pl.pallas_call(functools.partial(filter_kernel, sizes), out_shape=(jax.Sh...  75.6 us
    pallas_call x1, Pallas kernels, rotated(): pl.pallas_call(functools.partial(rotate_kernel, total_slots), out_shape=j...  8.92 us

profile of v3, /device:TPU:1, one launch (start us, length us, event | category | flops | bytes accessed | tf_op | source)
XLA Modules:
  0.0 84.6 jit_solution(2687301826830062941)
XLA Ops:
  0.0 75.6 %filter_gram.1 = (bf16[192,960]{1,0:T(8,128)(2,1)}, f32[192,256]{1,0:T(8,128)}) custom-call(f32[64]{0:T(128)} %table.1, s32[2,512]{1,0:T(2,128)} %conn.1, s32[4,120]{1,0:T(4,128)} %side.1, s32[2,64]{1,0:T(2,128)} %top.1, s32[1,960]{1,0:T(1,128)} %bitcast.1, bf16[192,960]{1,0:T(8,128)(2,1)} %x_hbm.1, bf16[2,512,512]{2,1,0:T(8,128)(2,1)} %k_hbm.1), custom_call_target="tpu_custom_call" | custom-call | tf_op jit(solution)/shard_map/filter_gram/pallas_call | solution.py:344
  75.6 8.9 %rotate.1 = bf16[192,960]{1,0:T(8,128)(2,1)} custom-call(f32[192,256]{1,0:T(8,128)} %get-tuple-element.7.gram, bf16[192,960]{1,0:T(8,128)(2,1)} %get-tuple-element.8.filt), custom_call_target="tpu_custom_call" | custom-call | tf_op jit(solution)/shard_map/rotate/pallas_call | solution.py:468
